TPU v7x, 32 devices: a whole 2x2x4 slice. The times are simulated.
32 devices in a mesh: batch: 4 (over y, core), ctx: 8 (over z, x).
Axes of the slice: x: 2, y: 2, z: 4, core: 2. Of those that a mesh axis runs over, the one named last changes fastest.
Arguments:
- activations: bfloat16 [8, 1024, 1024], P('batch', 'ctx'), parts along dimension 0, may hold values from -6 to 6
- project_in: bfloat16 [1024, 3072], replicated, may hold values from -0.1875 to 0.1875
- project_out: bfloat16 [1024, 1024], replicated, may hold values from -0.1875 to 0.1875
- norm_gain: float32 [1024], replicated, may hold values from 0.1 to 1.9
- regularizer: float32 [8, 128], replicated, may hold values from 0.5 to 16
- prior_gram: float32 [32, 128, 128], P('batch'), parts along dimension 0, as said below
- prior_value: float32 [32, 128, 128], P('batch'), parts along dimension 0, as said below
Outputs:
- layer_out: bfloat16 [8, 1024, 1024], P('batch', 'ctx'), parts along dimension 0
- next_gram: float32 [32, 128, 128], P('batch'), parts along dimension 0
- next_value: float32 [32, 128, 128], P('batch'), parts along dimension 0
There are 4 independent parts, one for each index of `batch`. A program takes and returns all parts, laid end to end along the dimension named above; an argument that names none is the same for every part. Nothing has to cross between parts.
Inputs may be any that keep to these rules, and one draw needn't show every extreme that they name: `prior_gram`: each head's matrix is symmetric positive definite. `prior_value`: summed over the same earlier tokens as prior_gram.
All inputs are finite; a program needn't handle non-finite values.
Results may differ from a plain program's by a relative error of at most 0.0055.
Values sent between devices are 32-bit elements; how exact they have to be, the bound alone decides.
A program may use at most 128 MiB of HBM per device.

v0:
```python
import jax
import jax.numpy as jnp
from jax import lax
from jax.sharding import PartitionSpec as P

HEADS = 8
DK = 128
ITERS = 8


epsilon = 1e-06
highest = lax.Precision.HIGHEST


def split_heads(packed):
    lead = packed.shape[:-1]
    parts = packed.reshape(lead + (3, HEADS, DK))
    parts = jnp.moveaxis(parts, -3, 0)
    parts = jnp.swapaxes(parts, -3, -2)
    return (parts[0], parts[1], parts[2])


def unit_rows(matrix):
    return matrix * lax.rsqrt(jnp.sum(matrix * matrix, -1, keepdims=True) + epsilon)


def mesa_block(queries, keys_unit, values, gram_state, value_state, regularizer):
    block_len = queries.shape[-2]
    row_index = lax.broadcasted_iota(jnp.int32, (block_len, block_len), 0)
    col_index = lax.broadcasted_iota(jnp.int32, (block_len, block_len), 1)
    causal = (row_index >= col_index).astype(jnp.float32)
    diag_reg = regularizer[:, None, :]
    solution = jnp.zeros_like(queries)
    residual = queries
    direction = queries
    norm_now = jnp.sum(residual * residual, -1, keepdims=True)
    for repeat in range(ITERS):
        apply_earlier = jnp.einsum("...ij,...tj->...ti", gram_state, direction, precision=highest)
        apply_scores = (
            jnp.einsum("...ti,...si->...ts", direction, keys_unit, precision=highest) * causal
        )
        gram_image = (
            apply_earlier
            + diag_reg * direction
            + jnp.einsum("...ts,...si->...ti", apply_scores, keys_unit, precision=highest)
        )
        step_size = norm_now / (jnp.sum(direction * gram_image, -1, keepdims=True) + epsilon)
        solution = solution + step_size * direction
        residual = residual - step_size * gram_image
        norm_next = jnp.sum(residual * residual, -1, keepdims=True)
        direction = residual + norm_next / (norm_now + epsilon) * direction
        norm_now = norm_next
    earlier = jnp.einsum("...ij,...tj->...ti", value_state, solution, precision=highest)
    scores = jnp.einsum("...ti,...si->...ts", solution, keys_unit, precision=highest) * causal
    return earlier + jnp.einsum("...ts,...si->...ti", scores, values, precision=highest)


def finish(mixed, norm_gain):
    scaled = mixed * lax.rsqrt(jnp.mean(mixed * mixed, -1, keepdims=True) + epsilon)
    scaled = jnp.swapaxes(scaled, -3, -2)
    merged = scaled.reshape(scaled.shape[:-2] + (HEADS * DK,))
    return (merged * norm_gain).astype(jnp.bfloat16)


def shards(activations, project_in, project_out, norm_gain, regularizer, prior_gram, prior_value):
    packed = jnp.einsum("std,de->ste", activations, project_in, preferred_element_type=jnp.float32)
    queries, keys_unit, values = split_heads(packed)
    queries = unit_rows(queries)
    keys_unit = unit_rows(keys_unit)
    gram_local = jnp.einsum("shti,shtj->shij", keys_unit, keys_unit, precision=highest)
    value_local = jnp.einsum("shti,shtj->shij", values, keys_unit, precision=highest)
    local = jnp.stack([gram_local, value_local], 1)
    position = lax.axis_index("ctx")
    piece = lax.all_gather(local[None], "ctx", axis=0, tiled=True)
    owners = lax.iota(jnp.int32, piece.shape[0])
    below = (owners < position).astype(jnp.float32)
    earlier = jnp.tensordot(below, piece, axes=1, precision=highest)
    totals = jnp.sum(piece, 0)
    earlier_segments = jnp.cumsum(totals, 0) - totals
    prefix = earlier_segments + earlier
    gram_start = prior_gram[None] + prefix[:, 0]
    value_start = prior_value[None] + prefix[:, 1]
    mixed = mesa_block(queries, keys_unit, values, gram_start, value_start, regularizer)
    normed = finish(mixed, norm_gain)
    layer_out = jnp.einsum(
        "std,de->ste", normed, project_out, preferred_element_type=jnp.float32
    ).astype(jnp.bfloat16)
    next_gram = prior_gram + jnp.sum(totals[:, 0], 0)
    next_value = prior_value + jnp.sum(totals[:, 1], 0)
    return (layer_out, next_gram, next_value)


def solution(mesh):
    placed = (
        P("batch", "ctx", None),
        P(),
        P(),
        P(),
        P(),
        P("batch", None, None),
        P("batch", None, None),
    )
    return jax.shard_map(
        shards,
        mesh=mesh,
        in_specs=placed,
        out_specs=(P("batch", "ctx", None), P("batch", None, None), P("batch", None, None)),
        check_vma=False,
    )
```

profile of v0, /device:TPU:0, one launch (start us, length us, event | category | flops | bytes accessed | tf_op | source)
XLA Modules:
  0.0 364.4 jit_solution(6835932239403860971)
XLA Ops:
  7.2 4.9 %fusion.2 = f32[2,128,3072]{2,1,0:T(8,128)S(1)} fusion(bf16[2,128,1024]{2,1,0:T(8,128)(2,1)} %param.7, bf16[1024,3072]{1,0:T(8,128)(2,1)} %param.8), kind=kOutput, calls=%fused_computation.2 | convolution fusion | flops 1610612736 | bytes 9961472 | tf_op jit(solution)/shard_map/std,de->ste/dot_general | solution.py:66
  12.1 2.2 copy.37
  14.3 3.6 copy.10
  17.9 1.7 multiply_reduce_fusion.17
  19.7 3.8 %convolution_bitcast_fusion = f32[2,1,8,128,128]{4,3,2,0,1:T(8,128)S(1)} fusion(f32[3,2,8,128,128]{3,4,2,1,0:T(8,128)} %bitcast.142, f32[2,8,128]{2,1,0:T(8,128)S(1)} %get-tuple-element.36), kind=kOutput, calls=%fused_computation.35 | convolution fusion | flops 402915328 | bytes 3153920 | tf_op jit(solution)/shard_map/shti,shtj->shij/dot_general | solution.py:71
  23.5 3.9 %convolution_bitcast_fusion.1 = f32[2,1,8,128,128]{4,3,2,0,1:T(8,128)S(1)} fusion(f32[3,2,8,128,128]{3,4,2,1,0:T(8,128)} %bitcast.143, f32[2,8,128]{2,1,0:T(8,128)S(1)} %get-tuple-element.36), kind=kOutput, calls=%fused_computation.36 | convolution fusion | flops 402915328 | bytes 2105344 | tf_op jit(solution)/shard_map/shti,shtj->shij/dot_general | solution.py:70
  27.4 1.5 pad_maximum_fusion
  28.9 3.4 convolution_multiply_fusion.8
  32.3 226.7 %all-gather.3.cloned.1.call-done = f32[16,2,8,128,128]{4,3,2,0,1:T(8,128)} async-done(((f32[2,2,8,128,128]{4,3,2,0,1:T(8,128)}), f32[16,2,8,128,128]{4,3,2,0,1:T(8,128)}) %all-gather.3.cloned.1.call-update) | async-done | bytes 16777232 | tf_op jit(solution)/shard_map/all_gather | solution.py:74
  259.0 23.7 %fusion = f32[1,2,2,8,128,128]{5,0,4,3,2,1:T(1,128)} fusion(f32[8,2,2,8,128,128]{5,4,3,1,0,2:T(8,128)} %bitcast.166, s32[]{:T(128)S(6)} %axis_index.12), kind=kOutput, calls=%fused_computation | convolution fusion | flops 50331656 | bytes 18874372 | tf_op jit(solution)/shard_map/dot_general | solution.py:77
  282.8 9.1 %reduce_sum.201 = f32[2,2,8,128,128]{4,3,2,0,1:T(8,128)} reduce(f32[8,2,2,8,128,128]{5,4,3,1,0,2:T(8,128)} %bitcast.167, f32[]{:T(128)} %constant.4.clone.1), dimensions={0}, to_apply=%region_3.0 | reduce | flops 3670016 | bytes 18874372 | tf_op jit(solution)/shard_map/reduce_sum | solution.py:78
  291.9 1.9 fusion.45
  293.8 0.3 copy-done.2
  294.1 0.6 copy-done.3
  294.8 0.5 bitcast_add_fusion
  295.3 0.5 copy-done.5
  295.8 0.1 fusion.14
  295.9 0.9 copy-done.1
  296.8 1.3 convolution_add_fusion.16
  298.1 2.4 multiply_reduce_fusion.14
  300.5 0.3 multiply_reduce_fusion.13
  300.8 0.2 multiply_add_fusion.7
  301.0 1.2 convolution_add_fusion.14
  302.2 1.9 convolution_multiply_fusion.7
  304.1 2.3 multiply_reduce_fusion.12
  306.4 0.2 multiply_reduce_fusion.11
  306.7 0.1 multiply_add_fusion.6
  306.8 1.4 convolution_add_fusion.12
  308.2 1.9 convolution_multiply_fusion.6
  310.1 2.3 multiply_reduce_fusion.10
  312.4 0.2 multiply_reduce_fusion.9
  312.7 0.1 multiply_add_fusion.5
  312.9 1.2 convolution_add_fusion.10
  314.0 1.9 convolution_multiply_fusion.5
  315.9 2.3 multiply_reduce_fusion.8
  318.3 0.2 multiply_reduce_fusion.7
  318.5 0.1 multiply_add_fusion.4
  318.7 1.2 convolution_add_fusion.8
  319.8 2.1 convolution_multiply_fusion.4
  321.9 2.3 multiply_reduce_fusion.6
  324.3 0.2 multiply_reduce_fusion.5
  324.5 0.1 multiply_add_fusion.3
  324.7 1.2 convolution_add_fusion.6
  325.8 1.9 convolution_multiply_fusion.3
  327.7 2.3 multiply_reduce_fusion.4
  330.1 0.2 multiply_reduce_fusion.3
  330.3 0.1 multiply_add_fusion.2
  330.5 1.2 convolution_add_fusion.4
  331.7 1.9 convolution_multiply_fusion.2
  333.5 2.3 multiply_reduce_fusion.2
  335.9 0.2 multiply_reduce_fusion.1
  336.1 0.6 multiply_add_fusion.1
  336.7 1.2 convolution_add_fusion.2
  337.8 1.9 convolution_multiply_fusion.1
  339.7 1.1 slice_reduce_fusion
  340.8 2.3 fusion.10
  343.1 1.4 multiply_add_fusion
  344.6 1.9 convolution_multiply_fusion
  346.5 1.1 fusion.12
  347.7 2.3 multiply_reduce_fusion
  350.1 1.3 copy.22
  351.5 2.1 add.323
  353.6 2.0 add.324
  355.7 1.5 fusion.7
  (35 shorter events, 0.3 us)
Async XLA Ops:
  7.2 348.5 %copy-start = (bf16[1024,1024]{1,0:T(8,128)(2,1)S(1)}, bf16[1024,1024]{1,0:T(8,128)(2,1)}, u32[]{:S(2)}) copy-start(bf16[1024,1024]{1,0:T(8,128)(2,1)} %param.9) | copy-start | bytes 6291460
  7.2 251.9 %all-gather.3.cloned.1.call-start = ((), (), s32[]{:S(2)}) async-start(), calls=%async_computation | async-start | bytes 18874368 | tf_op jit(solution)/shard_map/all_gather | solution.py:74
  291.9 2.2 copy-start.2
  291.9 2.9 copy-start.3
  294.8 1.0 copy-start.5
  294.8 2.1 copy-start.1
  294.8 2.1 copy-start.7
  344.6 1.9 copy-start.6
  350.1 5.5 %copy-start.8 = (f32[1024]{0:T(1024)S(1)}, f32[1024]{0:T(1024)}, u32[]{:S(2)}) copy-start(f32[1024]{0:T(1024)} %param.10) | copy-start | bytes 12292
  351.5 4.2 %copy-start.4 = (f32[2,128,1024]{2,1,0:T(8,128)S(1)}, f32[2,128,1024]{2,1,0:T(8,128)}, u32[]{:S(2)}) copy-start(f32[2,128,1024]{2,1,0:T(8,128)} %copy.22) | copy-start | bytes 3145732
Sparse Core Ops, SparseCore 0:
  29.0 229.9 all-gather.2
where the time goes:
time: 371 us; the launch traced here: 364 us
  waiting for transfers between devices  227 us (61%)
  matrix products  88.2 us (24%)
  other arithmetic  25 us (7%)
  between operations  15 us (4%)
  local copies, waits for them, and re-layouts  9.51 us (3%)
    all_gather x1, waiting for transfers between devices, shards(): piece = lax.all_gather(local[None], 'ctx', axis=0, tiled=True)  227 us
    dot_general x1, matrix products, shards(): earlier = jnp.tensordot(below, piece, axes=1, precision=highest)  23.7 us
    dot_general x8, matrix products, mesa_block(): jnp.einsum('...ts,...si->...ti', apply_scores, keys_unit, precision=highest)  18.5 us
    dot_general x8, matrix products, mesa_block(): jnp.einsum('...ti,...si->...ts', direction, keys_unit, precision=highest)  16.8 us
    dot_general x8, matrix products, mesa_block(): jnp.einsum('...ij,...tj->...ti', gram_state, direction, precision=highest)  9.66 us
    reduce_sum x1, other arithmetic, shards(): totals = jnp.sum(piece, 0)  9.12 us
  transfers between devices with their start and end apart: 1, of which 1 were waited for; matrix products, arithmetic and copies ran while one was open for 1% of the time, Pallas kernels for 0%

commit v1 on v0

v1 whole, which is shorter than its diff:
```python
import functools

import jax
import jax.numpy as jnp
from jax import lax
from jax.experimental import pallas as pl
from jax.experimental.pallas import tpu as pltpu
from jax.sharding import PartitionSpec as P

ITERS = 8
epsilon = 1e-06
f32, bf16 = jnp.float32, jnp.bfloat16
GROUP = 2


def halves(m):
    high = m.astype(bf16)
    return high, (m - high.astype(f32)).astype(bf16)


def left_of(m):
    return jnp.concatenate(halves(m), axis=1)


def right_of(m):
    high, low = halves(m)
    top = jnp.concatenate([high, low], axis=1)
    return jnp.concatenate([top, jnp.concatenate([high, jnp.zeros_like(low)], axis=1)], axis=0)


def product(left, right):
    n = right.shape[1] // 2
    wide = jnp.dot(left, right, preferred_element_type=f32)
    return wide[:, :n] + wide[:, n:]


def unit_rows(m):
    return m * lax.rsqrt(jnp.sum(m * m, -1, keepdims=True) + epsilon)


def kernel(
    near, far, heads, dk, segs,
    x_ref, win_ref, wout_ref, gain_ref, reg_ref, pg_ref, pv_ref,
    out_ref, ng_ref, nv_ref,
    win, wout, k_left, kt_left, vt_left, q_t,
    own_g, own_v, near_g, near_v, sum_g, sum_v, got_g, got_v, put_g, put_v,
    sol, res, dirn, rr_ref, ak_left, x_right, part, normed,
    copy_sem, near_send, near_recv, far_send, far_recv,
):
    width = heads * dk
    tok = x_ref.shape[0] // segs
    me = lax.axis_index("ctx")
    slow, fast = me // near, me % near
    first = (2 * slow >= far).astype(jnp.int32)

    copies = [
        pltpu.make_async_copy(
            win_ref.at[:, pl.ds(c * width, width)], win.at[:, pl.ds(c * width, width)], copy_sem.at[c]
        )
        for c in range(3)
    ]
    copies.append(pltpu.make_async_copy(wout_ref, wout, copy_sem.at[3]))
    for c in (1, 2, 0, 3):
        copies[c].start()

    barrier = pltpu.get_barrier_semaphore()
    for off in range(1, near):
        pl.semaphore_signal(barrier, inc=1, device_id={"ctx": slow * near + (fast + off) % near})

    @pl.when(slow > 0)
    def _():
        pl.semaphore_signal(barrier, inc=1, device_id={"ctx": me - near})

    @pl.when(slow < far - 1)
    def _():
        pl.semaphore_signal(barrier, inc=1, device_id={"ctx": me + near})

    ends = (slow > 0).astype(jnp.int32) + (slow < far - 1).astype(jnp.int32)
    pl.semaphore_wait(barrier, near - 1 + ends)

    own, nears, sums = (own_g, own_v), (near_g, near_v), (sum_g, sum_v)
    got, put = (got_g, got_v), (put_g, put_v)

    for kind in range(2):
        @pl.when(slow == 0)
        def _():
            got[kind][0] = jnp.zeros(got[kind].shape[1:], f32)

        @pl.when(slow == far - 1)
        def _():
            got[kind][1] = jnp.zeros(got[kind].shape[1:], f32)

    def near_copy(kind, h, off):
        slot = near - off - 1
        return pltpu.make_async_remote_copy(
            src_ref=own[kind].at[h],
            dst_ref=nears[kind].at[slot, h],
            send_sem=near_send.at[kind, slot, h],
            recv_sem=near_recv.at[kind, slot, h],
            device_id={"ctx": slow * near + (fast + off) % near},
        )

    def far_copy(kind, h, way, peer):
        return pltpu.make_async_remote_copy(
            src_ref=put[kind].at[way, h],
            dst_ref=got[kind].at[way, h],
            send_sem=far_send.at[kind, way, h],
            recv_sem=far_recv.at[kind, way, h],
            device_id={"ctx": peer},
        )

    def relay(kind, h, stage):
        way = first if stage == 0 else 1 - first
        step = 1 - 2 * way
        if stage == 0:
            total = own[kind][h]
            for off in range(1, near):
                near_copy(kind, h, off).wait_recv()
            for slot in range(near - 1):
                total = total + nears[kind][slot, h]
            sums[kind][h] = total
        before, after = slow - step, slow + step

        @pl.when((before >= 0) & (before < far))
        def _():
            far_copy(kind, h, way, me - step * near).wait_recv()

        @pl.when((after >= 0) & (after < far))
        def _():
            put[kind][way, h] = got[kind][way, h] + sums[kind][h]
            far_copy(kind, h, way, me + step * near).start()

    def prefix_and_total(kind, h):
        forward, backward = got[kind][0, h], got[kind][1, h]
        ahead = forward
        for slot in range(near - 1):
            weight = (fast + slot + 1 >= near).astype(f32)
            ahead = ahead + weight * nears[kind][slot, h]
        return ahead, forward + sums[kind][h] + backward

    row = lax.broadcasted_iota(jnp.int32, (dk, dk), 0)
    col = lax.broadcasted_iota(jnp.int32, (dk, dk), 1)
    lower, diagonal = row >= col, row == col
    trow = lax.broadcasted_iota(jnp.int32, (tok, tok), 0)
    tcol = lax.broadcasted_iota(jnp.int32, (tok, tok), 1)
    causal = trow <= tcol

    def unpack(p):
        body, tail = p[:dk], p[dk : dk + 1]
        turned = body.T
        zero = jnp.where(lower, body, turned)
        one = jnp.where(diagonal, tail, jnp.where(lower, turned, body))
        return zero, one

    copies[1].wait()

    def keys_step(p, c):
        at = pl.multiple_of(p * (GROUP * dk), GROUP * dk)
        keys = jnp.dot(x_ref[...], win[:, pl.ds(width + at, GROUP * dk)], preferred_element_type=f32)
        for g in range(GROUP):
            h = p * GROUP + g
            grams = []
            for s in range(segs):
                unit = unit_rows(keys[s * tok : (s + 1) * tok, g * dk : (g + 1) * dk])
                kt = left_of(unit.T)
                k_left[h, s] = left_of(unit)
                kt_left[h, s] = kt
                grams.append(product(kt, right_of(unit)))
            own_g[h, :dk] = jnp.where(lower, grams[0], grams[1])
            tail = jnp.sum(jnp.where(diagonal, grams[1], 0.0), axis=0, keepdims=True)
            own_g[h, dk:] = jnp.broadcast_to(tail, (8, dk))
            for off in range(1, near):
                near_copy(0, h, off).start()
        return c

    lax.fori_loop(0, heads // GROUP, keys_step, 0)
    copies[2].wait()
    copies[0].wait()

    def rest_step(p, c):
        at = pl.multiple_of(p * (GROUP * dk), GROUP * dk)
        values = jnp.dot(x_ref[...], win[:, pl.ds(2 * width + at, GROUP * dk)], preferred_element_type=f32)
        queries = jnp.dot(x_ref[...], win[:, pl.ds(at, GROUP * dk)], preferred_element_type=f32)
        for g in range(GROUP):
            h = p * GROUP + g
            for s in range(segs):
                rows, lanes = slice(s * tok, (s + 1) * tok), slice(g * dk, (g + 1) * dk)
                vt = left_of(values[rows, lanes].T)
                vt_left[h, s] = vt
                both = k_left[h, s]
                high, low = both[:, :dk], both[:, dk:]
                right = jnp.concatenate(
                    [both, jnp.concatenate([high, jnp.zeros_like(low)], axis=1)], axis=0
                )
                own_v[h, s * dk : (s + 1) * dk] = product(vt, right)
                q_t[h, s] = unit_rows(queries[rows, lanes]).T
            for off in range(1, near):
                near_copy(1, h, off).start()
        return c

    lax.fori_loop(0, heads // GROUP, rest_step, 0)

    def each(kind, stage, lo, count):
        def go(i, c):
            relay(kind, lo + i, stage)
            return c

        lax.fori_loop(0, count, go, 0)

    each(0, 0, 0, heads)
    each(0, 1, 0, GROUP)

    def solve_step(p, c):
        for g in range(GROUP):
            h = p * GROUP + g
            ahead, total = prefix_and_total(0, h)
            ahead0, ahead1 = unpack(ahead)
            total0, total1 = unpack(total)
            prior = pg_ref[h]
            ng_ref[h] = prior + (total0 + total1)
            diag = jnp.where(diagonal, reg_ref[pl.ds(h, 1), :], 0.0)
            base = prior + diag
            for s, gram in enumerate((base + ahead0, base + (total0 + ahead1))):
                i = g * segs + s
                ak_left[i, :dk] = left_of(gram)
                ak_left[i, dk:] = k_left[h, s]
                q = q_t[h, s]
                sol[i] = jnp.zeros_like(q)
                res[i] = q
                dirn[i] = q
                rr_ref[i] = jnp.broadcast_to(jnp.sum(q * q, 0, keepdims=True), rr_ref.shape[1:])

        def cg(it, c2):
            for g in range(GROUP):
                h = p * GROUP + g
                for s in range(segs):
                    i = g * segs + s
                    d = dirn[i]
                    y = product(ak_left[i], right_of(d))
                    scores = jnp.where(causal, y[dk:], 0.0)
                    image = y[:dk] + product(kt_left[h, s], right_of(scores))
                    rr = rr_ref[i, 0:1]
                    step = rr / (jnp.sum(d * image, 0, keepdims=True) + epsilon)
                    sol[i] = sol[i] + step * d
                    r = res[i] - step * image
                    res[i] = r
                    new = jnp.sum(r * r, 0, keepdims=True)
                    dirn[i] = r + (new / (rr + epsilon)) * d
                    rr_ref[i] = jnp.broadcast_to(new, rr_ref.shape[1:])
            return c2

        lax.fori_loop(0, ITERS, cg, 0)
        for g in range(GROUP):
            h = p * GROUP + g
            for s in range(segs):
                right = right_of(sol[g * segs + s])
                x_right[h, s] = right
                scores = jnp.where(causal, product(k_left[h, s], right), 0.0)
                part[h, s] = product(vt_left[h, s], right_of(scores))

        @pl.when(p < heads // GROUP - 1)
        def _():
            each(0, 1, (p + 1) * GROUP, GROUP)

        each(1, 0, p * GROUP, GROUP)

        @pl.when(p > 0)
        def _():
            each(1, 1, (p - 1) * GROUP, GROUP)

        return c

    lax.fori_loop(0, heads // GROUP, solve_step, 0)
    each(1, 1, heads - GROUP, GROUP)

    def mix_step(h, c):
        ahead, total = prefix_and_total(1, h)
        prior = pv_ref[h]
        total0 = total[:dk]
        nv_ref[h] = prior + (total0 + total[dk:])
        at = pl.multiple_of(h * dk, dk)
        for s, value in enumerate((prior + ahead[:dk], prior + (total0 + ahead[dk:]))):
            mixed = product(left_of(value), x_right[h, s]) + part[h, s]
            mean = jnp.sum(mixed * mixed, 0, keepdims=True) / dk
            scaled = (mixed * lax.rsqrt(mean + epsilon)).T * gain_ref[pl.ds(h, 1), :]
            normed[s * tok : (s + 1) * tok, pl.ds(at, dk)] = scaled.astype(bf16)
        return c

    lax.fori_loop(0, heads, mix_step, 0)
    copies[3].wait()
    out_ref[...] = jnp.dot(normed[...], wout[...], preferred_element_type=f32).astype(bf16)

    def drain(h, c):
        for kind in range(2):
            for off in range(1, near):
                near_copy(kind, h, off).wait_send()

            @pl.when(slow < far - 1)
            def _():
                far_copy(kind, h, 0, me + near).wait_send()

            @pl.when(slow > 0)
            def _():
                far_copy(kind, h, 1, me - near).wait_send()

        return c

    lax.fori_loop(0, heads, drain, 0)


def solution(mesh):
    n = mesh.shape["ctx"]
    near = 1 << ((n.bit_length() - 1) // 2)
    far = n // near

    def shards(activations, project_in, project_out, norm_gain, regularizer, prior_gram, prior_value):
        segs, tok, width = activations.shape
        heads, dk = regularizer.shape
        feats = heads * dk
        chains = GROUP * segs
        vmem = pl.BlockSpec(memory_space=pltpu.VMEM)
        hbm = pl.BlockSpec(memory_space=pl.ANY)
        gram, value = (dk + 8, dk), (segs * dk, dk)
        V = pltpu.VMEM
        D = pltpu.SemaphoreType.DMA
        slots = max(near - 1, 1)
        out, ng, nv = pl.pallas_call(
            functools.partial(kernel, near, far, heads, dk, segs),
            out_shape=(
                jax.ShapeDtypeStruct((segs * tok, width), bf16),
                jax.ShapeDtypeStruct(prior_gram.shape, f32),
                jax.ShapeDtypeStruct(prior_value.shape, f32),
            ),
            in_specs=[vmem, hbm, hbm, vmem, vmem, vmem, vmem],
            out_specs=(vmem, vmem, vmem),
            scratch_shapes=[
                V(project_in.shape, bf16),
                V(project_out.shape, bf16),
                V((heads, segs, tok, 2 * dk), bf16),
                V((heads, segs, dk, 2 * tok), bf16),
                V((heads, segs, dk, 2 * tok), bf16),
                V((heads, segs, dk, tok), f32),
                V((heads,) + gram, f32),
                V((heads,) + value, f32),
                V((slots, heads) + gram, f32),
                V((slots, heads) + value, f32),
                V((heads,) + gram, f32),
                V((heads,) + value, f32),
                V((2, heads) + gram, f32),
                V((2, heads) + value, f32),
                V((2, heads) + gram, f32),
                V((2, heads) + value, f32),
                V((chains, dk, tok), f32),
                V((chains, dk, tok), f32),
                V((chains, dk, tok), f32),
                V((chains, 8, tok), f32),
                V((chains, dk + tok, 2 * dk), bf16),
                V((heads, segs, 2 * dk, 2 * tok), bf16),
                V((heads, segs, dk, tok), f32),
                V((segs * tok, feats), bf16),
                D((4,)),
                D((2, slots, heads)),
                D((2, slots, heads)),
                D((2, 2, heads)),
                D((2, 2, heads)),
            ],
            compiler_params=pltpu.CompilerParams(
                collective_id=0, has_side_effects=True, vmem_limit_bytes=60 << 20
            ),
        )(
            activations.reshape(segs * tok, width),
            project_in,
            project_out,
            norm_gain.reshape(heads, dk),
            regularizer,
            prior_gram,
            prior_value,
        )
        return out.reshape(activations.shape), ng, nv

    return jax.shard_map(
        shards,
        mesh=mesh,
        in_specs=(
            P("batch", "ctx", None), P(), P(), P(), P(),
            P("batch", None, None), P("batch", None, None),
        ),
        out_specs=(P("batch", "ctx", None), P("batch", None, None), P("batch", None, None)),
        check_vma=False,
    )
```

time: 371 us -> 128 us (0.35); the launches traced: 364 us -> 127 us
  waiting for transfers between devices: 227 us -> 0 us
  Pallas kernels: 0 us -> 121 us
  matrix products: 88.2 us -> 0 us
  other arithmetic: 25 us -> 0 us
  between operations: 15 us -> 0.64 us
  local copies, waits for them, and re-layouts: 9.51 us -> 5.61 us
    all_gather x1 -> x0, waiting for transfers between devices: 227 us -> none  [shards(): piece = lax.all_gather(local[None], 'ctx', axis=0, tiled=True)]
    pallas_call x0 -> x1, Pallas kernels: none -> 121 us  [shards(): pl.pallas_call(functools.partial(kernel, near, far, heads, dk, segs), out...]
    dot_general x32 -> x0, matrix products: 88.2 us -> none  [the longest x1 23.7 us: shards(): earlier = jnp.tensordot(below, piece, axes=1, precision=highest)]
    reduce_sum x10 -> x0, other arithmetic: 13.5 us -> none  [the longest x1 9.12 us: shards(): totals = jnp.sum(piece, 0)]
    add x12 -> x0, other arithmetic: 7.77 us -> none  [the longest x1 2.14 us: shards(): next_gram = prior_gram + jnp.sum(totals[:, 0], 0)]
    reshape x2 -> x0, local copies, waits for them, and re-layouts: 4.91 us -> none  [the longest x1 3.59 us: split_heads(): parts = packed.reshape(lead + (3, HEADS, DK))]
  transfers between devices with their start and end apart: 1 -> 0, of which waited for: 1 -> 0; matrix products, arithmetic and copies ran while one was open for 1% -> 0% of each run, Pallas kernels for 0% -> 0%
where the time goes in v1:
time: 128 us; the launch traced here: 127 us
  Pallas kernels  121 us (95%)
  local copies, waits for them, and re-layouts  5.61 us (4%)
    pallas_call x1, Pallas kernels, shards(): pl.pallas_call(functools.partial(kernel, near, far, heads, dk, segs), out...  121 us
    unnamed x3, local copies, waits for them, and re-layouts  5.61 us

profile of v1, /device:TPU:0, one launch (start us, length us, event | category | flops | bytes accessed | tf_op | source)
XLA Modules:
  0.0 127.5 jit_solution(12496931803955721437)
XLA Ops:
  0.6 121.2 %shard_map.94 = (bf16[256,1024]{1,0:T(8,128)(2,1)}, f32[8,128,128]{2,1,0:T(8,128)}, f32[8,128,128]{2,1,0:T(8,128)}) custom-call(bf16[256,1024]{1,0:T(8,128)(2,1)} %bitcast.3, bf16[1024,3072]{1,0:T(8,128)(2,1)} %win_ref.1, bf16[1024,1024]{1,0:T(8,128)(2,1)} %wout_ref.1, f32[8,128]{1,0:T(8,128)} %bitcast.5, f32[8,128]{1,0:T(8,128)} %reg_ref.1, ...), custom_call_target="tpu_custom_call" | custom-call | tf_op jit(solution)/shard_map/pallas_call | solution.py:327
  121.9 1.9 %copy.13 = bf16[2,128,1024]{2,1,0:T(8,128)(2,1)} copy(bf16[2,128,1024]{2,1,0:T(8,128)(2,1)} %bitcast.4) | data formatting | bytes 1048576
  123.8 1.9 %copy.14 = f32[8,128,128]{2,1,0:T(8,128)} copy(f32[8,128,128]{2,1,0:T(8,128)} %get-tuple-element.13) | data formatting | bytes 1048576
  125.6 1.9 %copy.15 = f32[8,128,128]{2,1,0:T(8,128)} copy(f32[8,128,128]{2,1,0:T(8,128)} %get-tuple-element.14) | data formatting | bytes 1048576

commit v2 on v1

--- a/solution.py
+++ b/solution.py
@@ -120,17 +120,27 @@
                 total = total + nears[kind][slot, h]
             sums[kind][h] = total
         before, after = slow - step, slow + step
-
-        @pl.when((before >= 0) & (before < far))
+        passes = (after >= 0) & (after < far)
+        waits = (before >= 0) & (before < far)
+
+        @pl.when(waits & passes if stage else waits)
         def _():
             far_copy(kind, h, way, me - step * near).wait_recv()
 
-        @pl.when((after >= 0) & (after < far))
+        @pl.when(passes)
         def _():
             put[kind][way, h] = got[kind][way, h] + sums[kind][h]
             far_copy(kind, h, way, me + step * near).start()
 
     def prefix_and_total(kind, h):
+        way = 1 - first
+        step = 1 - 2 * way
+        before, after = slow - step, slow + step
+
+        @pl.when((before >= 0) & (before < far) & ((after < 0) | (after >= far)))
+        def _():
+            far_copy(kind, h, way, me - step * near).wait_recv()
+
         forward, backward = got[kind][0, h], got[kind][1, h]
         ahead = forward
         for slot in range(near - 1):
@@ -152,6 +162,7 @@
         one = jnp.where(diagonal, tail, jnp.where(lower, turned, body))
         return zero, one
 
+    early = heads // 2
     copies[1].wait()
 
     def keys_step(p, c):
@@ -207,8 +218,27 @@
 
         lax.fori_loop(0, count, go, 0)
 
-    each(0, 0, 0, heads)
+    each(0, 0, 0, early)
     each(0, 1, 0, GROUP)
+
+    def service(n):
+        @pl.when(n < heads - early)
+        def _():
+            relay(0, early + n, 0)
+
+        @pl.when(n < heads - GROUP)
+        def _():
+            relay(0, GROUP + n, 1)
+
+        @pl.when((n >= ITERS) & (n % 2 == 0) & (n < ITERS + 2 * heads))
+        def _():
+            relay(1, (n - ITERS) // 2, 0)
+
+        late = n - ITERS - 5
+
+        @pl.when((late >= 0) & (late % 2 == 0) & (late < 2 * heads))
+        def _():
+            relay(1, late // 2, 1)
 
     def solve_step(p, c):
         for g in range(GROUP):
@@ -247,6 +277,7 @@
                     new = jnp.sum(r * r, 0, keepdims=True)
                     dirn[i] = r + (new / (rr + epsilon)) * d
                     rr_ref[i] = jnp.broadcast_to(new, rr_ref.shape[1:])
+            service(p * ITERS + it)
             return c2
 
         lax.fori_loop(0, ITERS, cg, 0)
@@ -258,20 +289,9 @@
                 scores = jnp.where(causal, product(k_left[h, s], right), 0.0)
                 part[h, s] = product(vt_left[h, s], right_of(scores))
 
-        @pl.when(p < heads // GROUP - 1)
-        def _():
-            each(0, 1, (p + 1) * GROUP, GROUP)
-
-        each(1, 0, p * GROUP, GROUP)
-
-        @pl.when(p > 0)
-        def _():
-            each(1, 1, (p - 1) * GROUP, GROUP)
-
         return c
 
     lax.fori_loop(0, heads // GROUP, solve_step, 0)
-    each(1, 1, heads - GROUP, GROUP)
 
     def mix_step(h, c):
         ahead, total = prefix_and_total(1, h)

time: 128 us -> 83.3 us (0.65)
  the two profiles are of different devices: /device:TPU:0 before, /device:TPU:8 now
where the time goes in v2:
time: 83.3 us; the launch traced here: 83.1 us
  Pallas kernels  76.8 us (92%)
  local copies, waits for them, and re-layouts  5.61 us (7%)
    pallas_call x1, Pallas kernels, shards(): pl.pallas_call(functools.partial(kernel, near, far, heads, dk, segs), out...  76.8 us
    unnamed x3, local copies, waits for them, and re-layouts  5.61 us

profile of v2, /device:TPU:8, one launch (start us, length us, event | category | flops | bytes accessed | tf_op | source)
XLA Modules:
  0.0 83.1 jit_solution(3675582657562312581)
XLA Ops:
  0.6 76.8 %shard_map.94 = (bf16[256,1024]{1,0:T(8,128)(2,1)}, f32[8,128,128]{2,1,0:T(8,128)}, f32[8,128,128]{2,1,0:T(8,128)}) custom-call(bf16[256,1024]{1,0:T(8,128)(2,1)} %bitcast.3, bf16[1024,3072]{1,0:T(8,128)(2,1)} %win_ref.1, bf16[1024,1024]{1,0:T(8,128)(2,1)} %wout_ref.1, f32[8,128]{1,0:T(8,128)} %bitcast.5, f32[8,128]{1,0:T(8,128)} %reg_ref.1, ...), custom_call_target="tpu_custom_call" | custom-call | tf_op jit(solution)/shard_map/pallas_call | solution.py:347
  77.4 1.9 %copy.13 = bf16[2,128,1024]{2,1,0:T(8,128)(2,1)} copy(bf16[2,128,1024]{2,1,0:T(8,128)(2,1)} %bitcast.4) | data formatting | bytes 1048576
  79.3 1.9 %copy.14 = f32[8,128,128]{2,1,0:T(8,128)} copy(f32[8,128,128]{2,1,0:T(8,128)} %get-tuple-element.13) | data formatting | bytes 1048576
  81.2 1.9 %copy.15 = f32[8,128,128]{2,1,0:T(8,128)} copy(f32[8,128,128]{2,1,0:T(8,128)} %get-tuple-element.14) | data formatting | bytes 1048576
